TPU v7x, 32 devices: a whole 2x2x4 slice. The times are simulated.
32 devices in a mesh: txt: 4 (over z), aud: 8 (over y, x, core).
Axes of the slice: x: 2, y: 2, z: 4, core: 2. Of those that a mesh axis runs over, the one named last changes fastest.
Arguments:
- images: float32 [8192, 1024], P(('txt', 'aud')), may hold values from -2 to 2
- texts: float32 [64, 1024], P('txt'), may hold values from -2 to 2
- audio: float32 [32, 1024], P('aud'), may hold values from -2 to 2
- pos_text: int32 [8192], P(('txt', 'aud')), may hold values from 0 to 63
- pos_audio: int32 [8192], P(('txt', 'aud')), may hold values from 0 to 11
- logit_scale: float32 [1], replicated, may hold values from 1 to 4
- logit_bias: float32 [1], replicated, may hold values from -3 to -1
Outputs:
- grad_images: float32 [8192, 1024], P(('txt', 'aud'))
- grad_texts: float32 [64, 1024], P('txt')
- grad_audio: float32 [32, 1024], P('aud')
All inputs are finite; a program needn't handle non-finite values.
Results may differ from a plain program's by a relative error of at most 0.0044.
Values sent between devices are 32-bit elements; how exact they have to be, the bound alone decides.
A program may use at most 64 MiB of HBM per device.

v0:
```python
import jax
import jax.numpy as jnp
from jax import lax
from jax.sharding import PartitionSpec as P

HOPS = 2


def from_behind(shard, axis, by):
    size = lax.axis_size(axis)
    return lax.ppermute(shard, axis, [(i, (i + by) % size) for i in range(size)])


def block_terms(image_half, text_piece, window, first_row, pos_text, pos_audio, temper, offset):
    row_count = text_piece.shape[0]
    slot_count = window.shape[0]
    products = (
        (text_piece[:, None, :] * window[None, :, :])
        .reshape(row_count * slot_count, -1)
        .astype(jnp.bfloat16)
    )
    logits = (
        temper
        * lax.dot_general(
            image_half, products, (((1,), (1,)), ((), ())), preferred_element_type=jnp.float32
        )
        + offset
    )
    columns = jnp.arange(row_count * slot_count, dtype=jnp.int32)
    text_of = first_row + columns // slot_count
    slot_of = columns % slot_count
    positive = (text_of[None, :] == pos_text[:, None]) & (slot_of[None, :] == pos_audio[:, None])
    slope = ((jax.nn.sigmoid(logits) - positive.astype(jnp.float32)) * temper).astype(jnp.bfloat16)
    grad_image = jnp.dot(slope, products, preferred_element_type=jnp.float32)
    grad_prod = lax.dot_general(
        slope, image_half, (((0,), (0,)), ((), ())), preferred_element_type=jnp.float32
    )
    grad_prod = grad_prod.reshape(row_count, slot_count, -1)
    grad_piece = jnp.sum(grad_prod * window[None, :, :], axis=1)
    grad_window = jnp.sum(grad_prod * text_piece[:, None, :], axis=0)
    return (grad_image, grad_piece, grad_window)


def send_home(grad_window, block_rows):
    carried = grad_window[HOPS * block_rows :]
    for number in range(HOPS):
        level = HOPS - 1 - number
        carried = (
            from_behind(carried, "aud", 1)
            + grad_window[level * block_rows : (level + 1) * block_rows]
        )
    return carried


def shards(images, texts, audio, pos_text, pos_audio, logit_scale, logit_bias):
    temper = logit_scale[0]
    offset = logit_bias[0]
    block_rows = audio.shape[0]
    text_rows = texts.shape[0]
    pieces = [audio]
    current = audio
    for number in range(HOPS):
        current = from_behind(current, "aud", -1)
        pieces.append(current)
    window = jnp.concatenate(pieces, axis=0)
    image_half = images.astype(jnp.bfloat16)
    cycle_size = lax.axis_size("txt")
    position = lax.axis_index("txt")
    empty_image = jnp.zeros(images.shape, jnp.float32)
    empty_window = jnp.zeros(window.shape, jnp.float32)

    def advance(turn_index, state):
        held_text, held_grad, grad_image, grad_window = state
        owner = (position - turn_index) % cycle_size
        first = owner * text_rows
        more_image, more_piece, more_window = block_terms(
            image_half, held_text, window, first, pos_text, pos_audio, temper, offset
        )
        held_text, held_grad = from_behind((held_text, held_grad + more_piece), "txt", 1)
        return (held_text, held_grad, grad_image + more_image, grad_window + more_window)

    start_state = (texts, jnp.zeros(texts.shape, jnp.float32), empty_image, empty_window)
    final_state = lax.fori_loop(0, cycle_size, advance, start_state)
    grad_local_text = final_state[1]
    grad_images = final_state[2]
    grad_window = final_state[3]
    grad_texts = lax.psum(grad_local_text, "aud")
    returned = send_home(grad_window, block_rows)
    grad_audio = lax.psum(returned, "txt")
    return (grad_images, grad_texts, grad_audio)


def solution(mesh):
    placed = (
        P(("txt", "aud"), None),
        P("txt", None),
        P("aud", None),
        P(("txt", "aud")),
        P(("txt", "aud")),
        P(),
        P(),
    )
    return jax.shard_map(
        shards,
        mesh=mesh,
        in_specs=placed,
        out_specs=(P(("txt", "aud"), None), P("txt", None), P("aud", None)),
        check_vma=False,
    )
```

profile of v0, /device:TPU:0, one launch (start us, length us, event | category | flops | bytes accessed | tf_op | source)
XLA Modules:
  0.0 129.0 jit_solution(8001635966012682799)
XLA Ops:
  7.2 1.5 %copy.28 = f32[16,1024]{1,0:T(8,128)} copy(f32[16,1024]{1,0:T(8,128)} %param.10) | data formatting | bytes 131072
  8.7 3.4 %collective-permute-start.2 = (f32[4,1024]{1,0:T(4,128)S(1)}, f32[4,1024]{1,0:T(4,128)S(1)}, u32[]{:S(2)}, u32[]{:S(2)}) collective-permute-start(f32[4,1024]{1,0:T(4,128)S(1)} %copy-done.3), channel_id=1, source_target_pairs={{0,7},{1,0},{2,1},{3,2},{4,3},{5,4},{6,5},{7,6},{8,15},{9,8},{10,9... | collective-permute-start | bytes 49160 | tf_op jit(solution)/shard_map/ppermute | solution.py:11
  12.1 1.4 %collective-permute-done.2 = f32[4,1024]{1,0:T(4,128)S(1)} collective-permute-done((f32[4,1024]{1,0:T(4,128)S(1)}, f32[4,1024]{1,0:T(4,128)S(1)}, u32[]{:S(2)}, u32[]{:S(2)}) %collective-permute-start.2) | collective-permute-done | bytes 16416 | tf_op jit(solution)/shard_map/ppermute | solution.py:11
  13.5 2.6 %collective-permute-start.3 = (f32[4,1024]{1,0:T(4,128)S(1)}, f32[4,1024]{1,0:T(4,128)S(1)}, u32[]{:S(2)}, u32[]{:S(2)}) collective-permute-start(f32[4,1024]{1,0:T(4,128)S(1)} %collective-permute-done.2), channel_id=1, source_target_pairs={{0,7},{1,0},{2,1},{3,2},{4,3},{5,4},{6,5},{7,6},{8,15},{9,8},{10,9... | collective-permute-start | bytes 49160 | tf_op jit(solution)/shard_map/ppermute | solution.py:11
  16.1 1.3 %convert_element_type.39 = bf16[256,1024]{1,0:T(8,128)(2,1)S(1)} convert(f32[256,1024]{1,0:T(8,128)} %param.9) | non-fusion elementwise | flops 262144 | bytes 1572864 | tf_op jit(solution)/shard_map/convert_element_type | solution.py:66
  17.6 0.6 broadcast_in_dim.29
  18.3 43.6 %while.23 = (s32[]{:T(128)}, f32[16,1024]{1,0:T(8,128)}, f32[16,1024]{1,0:T(8,128)}, f32[256,1024]{1,0:T(8,128)S(1)}, f32[12,1024]{1,0:T(8,128)}, /*index=5*/f32...) while((s32[]{:T(128)}, f32[16,1024]{1,0:T(8,128)}, ...), condition=%wide.region_3.4_spmd.clone, body=%wide.region_0.3_spmd.clone.sunk | while | flops 304298432 | bytes 14095809 | solution.py:83
  18.3 0.9 copy.16
  19.2 1.6 %collective-permute-start = (f32[16,1024]{1,0:T(8,128)S(1)}, f32[16,1024]{1,0:T(8,128)}, u32[]{:S(2)}, u32[]{:S(2)}) collective-permute-start(f32[16,1024]{1,0:T(8,128)S(1)} %copy.16), channel_id=1, source_target_pairs={{0,8},{8,16},{16,24},{24,0},{1,9},{9,17},{17,25},{25,1},{2,10},{10... | collective-permute-start | bytes 196616 | tf_op jit(solution)/shard_map/while/body/eval_jaxpr/ppermute | solution.py:11
  20.9 1.7 %fusion.33 = bf16[256,192]{0,1:T(8,128)(2,1)S(1)} fusion(bf16[192,1024]{1,0:T(8,128)(2,1)S(1)} %convert_element_type.54, bf16[256,1024]{1,0:T(8,128)(2,1)S(1)} %get-tuple-element.525, f32[]{:T(128)} %get-tuple-element.523, s32[256]{0:T(256)S(1)} %get-tuple-element.529, s32[256]{0:T(256)S(1)} %get-tuple-element.528, f32[]{:T(128)} %get-tuple-element.526, ...), kind=kOutput, calls=%fused_computation.10.clone.1 | convolution fusion | flops 101253120 | bytes 1019400 | tf_op jit(solution)/shard_map/while/body/eval_jaxpr/dot_general | solution.py:24
  23.0 0.3 multiply_reduce_fusion.3
  23.3 0.8 add.228
  24.1 1.6 %collective-permute-start.1 = (f32[16,1024]{1,0:T(8,128)S(1)}, f32[16,1024]{1,0:T(8,128)}, u32[]{:S(2)}, u32[]{:S(2)}) collective-permute-start(f32[16,1024]{1,0:T(8,128)S(1)} %add.228), channel_id=1, source_target_pairs={{0,8},{8,16},{16,24},{24,0},{1,9},{9,17},{17,25},{25,1},{2,10},{10... | collective-permute-start | bytes 196616 | tf_op jit(solution)/shard_map/while/body/eval_jaxpr/ppermute | solution.py:11
  25.8 0.4 convolution_add_fusion.2
  26.2 0.7 select_add_fusion.2
  26.8 3.5 %collective-permute-done.1 = f32[16,1024]{1,0:T(8,128)} collective-permute-done((f32[16,1024]{1,0:T(8,128)S(1)}, f32[16,1024]{1,0:T(8,128)}, u32[]{:S(2)}, u32[]{:S(2)}) %collective-permute-start.1) | collective-permute-done | bytes 65568 | tf_op jit(solution)/shard_map/while/body/eval_jaxpr/ppermute | solution.py:11
  30.4 0.9 copy.16
  31.4 1.7 %fusion.33 = bf16[256,192]{0,1:T(8,128)(2,1)S(1)} fusion(bf16[192,1024]{1,0:T(8,128)(2,1)S(1)} %convert_element_type.54, bf16[256,1024]{1,0:T(8,128)(2,1)S(1)} %get-tuple-element.525, f32[]{:T(128)} %get-tuple-element.523, s32[256]{0:T(256)S(1)} %get-tuple-element.529, s32[256]{0:T(256)S(1)} %get-tuple-element.528, f32[]{:T(128)} %get-tuple-element.526, ...), kind=kOutput, calls=%fused_computation.10.clone.1 | convolution fusion | flops 101253120 | bytes 1019400 | tf_op jit(solution)/shard_map/while/body/eval_jaxpr/dot_general | solution.py:24
  33.5 0.3 multiply_reduce_fusion.3
  33.8 0.8 add.228
  34.6 1.4 %collective-permute-start.1 = (f32[16,1024]{1,0:T(8,128)S(1)}, f32[16,1024]{1,0:T(8,128)}, u32[]{:S(2)}, u32[]{:S(2)}) collective-permute-start(f32[16,1024]{1,0:T(8,128)S(1)} %add.228), channel_id=1, source_target_pairs={{0,8},{8,16},{16,24},{24,0},{1,9},{9,17},{17,25},{25,1},{2,10},{10... | collective-permute-start | bytes 196616 | tf_op jit(solution)/shard_map/while/body/eval_jaxpr/ppermute | solution.py:11
  36.0 0.4 convolution_add_fusion.2
  36.4 1.5 %select_add_fusion.2 = f32[12,1024]{1,0:T(8,128)} fusion(f32[12,1024]{1,0:T(8,128)S(1)} %get-tuple-element.483, f32[12,1024]{1,0:T(8,128)} %get-tuple-element.505, pred[]{:T(512)S(6)} %compare.5), kind=kLoop, calls=%fused_computation.14.clone.1 | loop fusion | flops 24576 | bytes 147457 | tf_op jit(solution)/shard_map/while/body/eval_jaxpr/add | solution.py:80
  38.0 2.9 %collective-permute-done.1 = f32[16,1024]{1,0:T(8,128)} collective-permute-done((f32[16,1024]{1,0:T(8,128)S(1)}, f32[16,1024]{1,0:T(8,128)}, u32[]{:S(2)}, u32[]{:S(2)}) %collective-permute-start.1) | collective-permute-done | bytes 65568 | tf_op jit(solution)/shard_map/while/body/eval_jaxpr/ppermute | solution.py:11
  40.9 0.9 copy.16
  42.0 1.7 %fusion.33 = bf16[256,192]{0,1:T(8,128)(2,1)S(1)} fusion(bf16[192,1024]{1,0:T(8,128)(2,1)S(1)} %convert_element_type.54, bf16[256,1024]{1,0:T(8,128)(2,1)S(1)} %get-tuple-element.525, f32[]{:T(128)} %get-tuple-element.523, s32[256]{0:T(256)S(1)} %get-tuple-element.529, s32[256]{0:T(256)S(1)} %get-tuple-element.528, f32[]{:T(128)} %get-tuple-element.526, ...), kind=kOutput, calls=%fused_computation.10.clone.1 | convolution fusion | flops 101253120 | bytes 1019400 | tf_op jit(solution)/shard_map/while/body/eval_jaxpr/dot_general | solution.py:24
  44.0 0.3 multiply_reduce_fusion.3
  44.3 0.8 add.228
  45.1 1.1 collective-permute-start.1
  46.2 0.4 convolution_add_fusion.2
  46.6 1.5 %select_add_fusion.2 = f32[12,1024]{1,0:T(8,128)} fusion(f32[12,1024]{1,0:T(8,128)S(1)} %get-tuple-element.483, f32[12,1024]{1,0:T(8,128)} %get-tuple-element.505, pred[]{:T(512)S(6)} %compare.5), kind=kLoop, calls=%fused_computation.14.clone.1 | loop fusion | flops 24576 | bytes 147457 | tf_op jit(solution)/shard_map/while/body/eval_jaxpr/add | solution.py:80
  48.2 3.2 %collective-permute-done.1 = f32[16,1024]{1,0:T(8,128)} collective-permute-done((f32[16,1024]{1,0:T(8,128)S(1)}, f32[16,1024]{1,0:T(8,128)}, u32[]{:S(2)}, u32[]{:S(2)}) %collective-permute-start.1) | collective-permute-done | bytes 65568 | tf_op jit(solution)/shard_map/while/body/eval_jaxpr/ppermute | solution.py:11
  51.4 0.9 copy.16
  52.5 1.7 %fusion.33 = bf16[256,192]{0,1:T(8,128)(2,1)S(1)} fusion(bf16[192,1024]{1,0:T(8,128)(2,1)S(1)} %convert_element_type.54, bf16[256,1024]{1,0:T(8,128)(2,1)S(1)} %get-tuple-element.525, f32[]{:T(128)} %get-tuple-element.523, s32[256]{0:T(256)S(1)} %get-tuple-element.529, s32[256]{0:T(256)S(1)} %get-tuple-element.528, f32[]{:T(128)} %get-tuple-element.526, ...), kind=kOutput, calls=%fused_computation.10.clone.1 | convolution fusion | flops 101253120 | bytes 1019400 | tf_op jit(solution)/shard_map/while/body/eval_jaxpr/dot_general | solution.py:24
  54.5 0.3 multiply_reduce_fusion.3
  54.8 0.8 add.228
  55.7 2.3 %collective-permute-start.1 = (f32[16,1024]{1,0:T(8,128)S(1)}, f32[16,1024]{1,0:T(8,128)}, u32[]{:S(2)}, u32[]{:S(2)}) collective-permute-start(f32[16,1024]{1,0:T(8,128)S(1)} %add.228), channel_id=1, source_target_pairs={{0,8},{8,16},{16,24},{24,0},{1,9},{9,17},{17,25},{25,1},{2,10},{10... | collective-permute-start | bytes 196616 | tf_op jit(solution)/shard_map/while/body/eval_jaxpr/ppermute | solution.py:11
  57.9 0.4 convolution_add_fusion.2
  58.3 1.5 %select_add_fusion.2 = f32[12,1024]{1,0:T(8,128)} fusion(f32[12,1024]{1,0:T(8,128)S(1)} %get-tuple-element.483, f32[12,1024]{1,0:T(8,128)} %get-tuple-element.505, pred[]{:T(512)S(6)} %compare.5), kind=kLoop, calls=%fused_computation.14.clone.1 | loop fusion | flops 24576 | bytes 147457 | tf_op jit(solution)/shard_map/while/body/eval_jaxpr/add | solution.py:80
  59.8 2.1 %collective-permute-done.1 = f32[16,1024]{1,0:T(8,128)} collective-permute-done((f32[16,1024]{1,0:T(8,128)S(1)}, f32[16,1024]{1,0:T(8,128)}, u32[]{:S(2)}, u32[]{:S(2)}) %collective-permute-start.1) | collective-permute-done | bytes 65568 | tf_op jit(solution)/shard_map/while/body/eval_jaxpr/ppermute | solution.py:11
  61.9 0.8 slice.9
  62.7 4.1 %collective-permute-done.4 = f32[4,1024]{1,0:T(4,128)S(1)} collective-permute-done((f32[4,1024]{1,0:T(4,128)S(1)}, f32[4,1024]{1,0:T(4,128)S(1)}, u32[]{:S(2)}, u32[]{:S(2)}) %collective-permute-start.4) | collective-permute-done | bytes 16416 | tf_op jit(solution)/shard_map/ppermute | solution.py:11
  66.7 0.8 slice_add_fusion.1
  67.5 4.0 %collective-permute-done.5 = f32[4,1024]{1,0:T(4,128)S(1)} collective-permute-done((f32[4,1024]{1,0:T(4,128)S(1)}, f32[4,1024]{1,0:T(4,128)S(1)}, u32[]{:S(2)}, u32[]{:S(2)}) %collective-permute-start.5) | collective-permute-done | bytes 16416 | tf_op jit(solution)/shard_map/ppermute | solution.py:11
  71.5 0.8 slice_add_fusion
  72.3 18.0 %psum.15 = f32[4,1024]{1,0:T(4,128)} all-reduce(f32[4,1024]{1,0:T(4,128)S(1)} %slice_add_fusion), channel_id=1, replica_groups=mesh['txt'=4,'aud'=8] {'txt'}, use_global_device_ids=true, to_apply=%region_5.6 | all-reduce | flops 4096 | bytes 32768 | tf_op jit(solution)/shard_map/psum | solution.py:89
  90.3 30.4 %all-reduce.2.cloned.1.call-done = f32[16,1024]{1,0:T(8,128)} async-done(((f32[16,1024]{1,0:T(8,128)}), f32[16,1024]{1,0:T(8,128)}) %all-reduce.2.cloned.1.call-update) | async-done | bytes 65552 | tf_op jit(solution)/shard_map/psum | solution.py:87
  120.7 1.5 %copy.29 = f32[16,1024]{1,0:T(8,128)} copy(f32[16,1024]{1,0:T(8,128)} %all-reduce.2.cloned.1.call-done) | data formatting | bytes 131072
  (59 shorter events, 2.5 us)
Async XLA Ops:
  7.2 1.5 %copy-start.3 = (f32[4,1024]{1,0:T(4,128)S(1)}, f32[4,1024]{1,0:T(4,128)}, u32[]{:S(2)}) copy-start(f32[4,1024]{1,0:T(4,128)} %param.11) | copy-start | bytes 49156
  7.2 113.5 %all-reduce.2.cloned.1.call-start = ((), (), s32[]{:S(2)}) async-start(), calls=%async_computation | async-start | bytes 131072 | tf_op jit(solution)/shard_map/psum | solution.py:87
  8.7 4.8 %collective-permute-start.2 = (f32[4,1024]{1,0:T(4,128)S(1)}, f32[4,1024]{1,0:T(4,128)S(1)}, u32[]{:S(2)}, u32[]{:S(2)}) collective-permute-start(f32[4,1024]{1,0:T(4,128)S(1)} %copy-done.3), channel_id=1, source_target_pairs={{0,7},{1,0},{2,1},{3,2},{4,3},{5,4},{6,5},{7,6},{8,15},{9,8},{10,9... | collective-permute-start | bytes 49160 | tf_op jit(solution)/shard_map/ppermute | solution.py:11
  13.5 4.1 %collective-permute-start.3 = (f32[4,1024]{1,0:T(4,128)S(1)}, f32[4,1024]{1,0:T(4,128)S(1)}, u32[]{:S(2)}, u32[]{:S(2)}) collective-permute-start(f32[4,1024]{1,0:T(4,128)S(1)} %collective-permute-done.2), channel_id=1, source_target_pairs={{0,7},{1,0},{2,1},{3,2},{4,3},{5,4},{6,5},{7,6},{8,15},{9,8},{10,9... | collective-permute-start | bytes 49160 | tf_op jit(solution)/shard_map/ppermute | solution.py:11
  17.6 0.7 copy-start.4
  17.6 0.7 copy-start.5
  18.3 4.3 %copy-start.1 = (bf16[256,1024]{1,0:T(8,128)(2,1)}, bf16[256,1024]{1,0:T(8,128)(2,1)S(1)}, u32[]{:S(2)}) copy-start(bf16[256,1024]{1,0:T(8,128)(2,1)S(1)} %get-tuple-element.525) | copy-start | bytes 1572868 | tf_op jit(solution)/shard_map/while
  19.2 7.7 %collective-permute-start = (f32[16,1024]{1,0:T(8,128)S(1)}, f32[16,1024]{1,0:T(8,128)}, u32[]{:S(2)}, u32[]{:S(2)}) collective-permute-start(f32[16,1024]{1,0:T(8,128)S(1)} %copy.16), channel_id=1, source_target_pairs={{0,8},{8,16},{16,24},{24,0},{1,9},{9,17},{17,25},{25,1},{2,10},{10... | collective-permute-start | bytes 196616 | tf_op jit(solution)/shard_map/while/body/eval_jaxpr/ppermute | solution.py:11
  24.1 6.2 %collective-permute-start.1 = (f32[16,1024]{1,0:T(8,128)S(1)}, f32[16,1024]{1,0:T(8,128)}, u32[]{:S(2)}, u32[]{:S(2)}) collective-permute-start(f32[16,1024]{1,0:T(8,128)S(1)} %add.228), channel_id=1, source_target_pairs={{0,8},{8,16},{16,24},{24,0},{1,9},{9,17},{17,25},{25,1},{2,10},{10... | collective-permute-start | bytes 196616 | tf_op jit(solution)/shard_map/while/body/eval_jaxpr/ppermute | solution.py:11
  25.8 4.6 %copy-start.2 = (bf16[256,1024]{1,0:T(8,128)(2,1)S(1)}, bf16[256,1024]{1,0:T(8,128)(2,1)}, u32[]{:S(2)}) copy-start(bf16[256,1024]{1,0:T(8,128)(2,1)} %copy-done.1) | copy-start | bytes 1572868 | tf_op jit(solution)/shard_map/while
  30.4 2.8 %copy-start.1 = (bf16[256,1024]{1,0:T(8,128)(2,1)}, bf16[256,1024]{1,0:T(8,128)(2,1)S(1)}, u32[]{:S(2)}) copy-start(bf16[256,1024]{1,0:T(8,128)(2,1)S(1)} %get-tuple-element.525) | copy-start | bytes 1572868 | tf_op jit(solution)/shard_map/while
  31.2 6.7 %collective-permute-start = (f32[16,1024]{1,0:T(8,128)S(1)}, f32[16,1024]{1,0:T(8,128)}, u32[]{:S(2)}, u32[]{:S(2)}) collective-permute-start(f32[16,1024]{1,0:T(8,128)S(1)} %copy.16), channel_id=1, source_target_pairs={{0,8},{8,16},{16,24},{24,0},{1,9},{9,17},{17,25},{25,1},{2,10},{10... | collective-permute-start | bytes 196616 | tf_op jit(solution)/shard_map/while/body/eval_jaxpr/ppermute | solution.py:11
  34.6 6.2 %collective-permute-start.1 = (f32[16,1024]{1,0:T(8,128)S(1)}, f32[16,1024]{1,0:T(8,128)}, u32[]{:S(2)}, u32[]{:S(2)}) collective-permute-start(f32[16,1024]{1,0:T(8,128)S(1)} %add.228), channel_id=1, source_target_pairs={{0,8},{8,16},{16,24},{24,0},{1,9},{9,17},{17,25},{25,1},{2,10},{10... | collective-permute-start | bytes 196616 | tf_op jit(solution)/shard_map/while/body/eval_jaxpr/ppermute | solution.py:11
  36.0 4.8 %copy-start.2 = (bf16[256,1024]{1,0:T(8,128)(2,1)S(1)}, bf16[256,1024]{1,0:T(8,128)(2,1)}, u32[]{:S(2)}) copy-start(bf16[256,1024]{1,0:T(8,128)(2,1)} %copy-done.1) | copy-start | bytes 1572868 | tf_op jit(solution)/shard_map/while
  40.9 2.8 %copy-start.1 = (bf16[256,1024]{1,0:T(8,128)(2,1)}, bf16[256,1024]{1,0:T(8,128)(2,1)S(1)}, u32[]{:S(2)}) copy-start(bf16[256,1024]{1,0:T(8,128)(2,1)S(1)} %get-tuple-element.525) | copy-start | bytes 1572868 | tf_op jit(solution)/shard_map/while
  41.8 6.4 %collective-permute-start = (f32[16,1024]{1,0:T(8,128)S(1)}, f32[16,1024]{1,0:T(8,128)}, u32[]{:S(2)}, u32[]{:S(2)}) collective-permute-start(f32[16,1024]{1,0:T(8,128)S(1)} %copy.16), channel_id=1, source_target_pairs={{0,8},{8,16},{16,24},{24,0},{1,9},{9,17},{17,25},{25,1},{2,10},{10... | collective-permute-start | bytes 196616 | tf_op jit(solution)/shard_map/while/body/eval_jaxpr/ppermute | solution.py:11
  45.1 6.2 %collective-permute-start.1 = (f32[16,1024]{1,0:T(8,128)S(1)}, f32[16,1024]{1,0:T(8,128)}, u32[]{:S(2)}, u32[]{:S(2)}) collective-permute-start(f32[16,1024]{1,0:T(8,128)S(1)} %add.228), channel_id=1, source_target_pairs={{0,8},{8,16},{16,24},{24,0},{1,9},{9,17},{17,25},{25,1},{2,10},{10... | collective-permute-start | bytes 196616 | tf_op jit(solution)/shard_map/while/body/eval_jaxpr/ppermute | solution.py:11
  46.2 5.2 %copy-start.2 = (bf16[256,1024]{1,0:T(8,128)(2,1)S(1)}, bf16[256,1024]{1,0:T(8,128)(2,1)}, u32[]{:S(2)}) copy-start(bf16[256,1024]{1,0:T(8,128)(2,1)} %copy-done.1) | copy-start | bytes 1572868 | tf_op jit(solution)/shard_map/while
  51.4 2.8 %copy-start.1 = (bf16[256,1024]{1,0:T(8,128)(2,1)}, bf16[256,1024]{1,0:T(8,128)(2,1)S(1)}, u32[]{:S(2)}) copy-start(bf16[256,1024]{1,0:T(8,128)(2,1)S(1)} %get-tuple-element.525) | copy-start | bytes 1572868 | tf_op jit(solution)/shard_map/while
  52.3 7.5 %collective-permute-start = (f32[16,1024]{1,0:T(8,128)S(1)}, f32[16,1024]{1,0:T(8,128)}, u32[]{:S(2)}, u32[]{:S(2)}) collective-permute-start(f32[16,1024]{1,0:T(8,128)S(1)} %copy.16), channel_id=1, source_target_pairs={{0,8},{8,16},{16,24},{24,0},{1,9},{9,17},{17,25},{25,1},{2,10},{10... | collective-permute-start | bytes 196616 | tf_op jit(solution)/shard_map/while/body/eval_jaxpr/ppermute | solution.py:11
  55.7 6.2 %collective-permute-start.1 = (f32[16,1024]{1,0:T(8,128)S(1)}, f32[16,1024]{1,0:T(8,128)}, u32[]{:S(2)}, u32[]{:S(2)}) collective-permute-start(f32[16,1024]{1,0:T(8,128)S(1)} %add.228), channel_id=1, source_target_pairs={{0,8},{8,16},{16,24},{24,0},{1,9},{9,17},{17,25},{25,1},{2,10},{10... | collective-permute-start | bytes 196616 | tf_op jit(solution)/shard_map/while/body/eval_jaxpr/ppermute | solution.py:11
  57.9 4.0 %copy-start.2 = (bf16[256,1024]{1,0:T(8,128)(2,1)S(1)}, bf16[256,1024]{1,0:T(8,128)(2,1)}, u32[]{:S(2)}) copy-start(bf16[256,1024]{1,0:T(8,128)(2,1)} %copy-done.1) | copy-start | bytes 1572868 | tf_op jit(solution)/shard_map/while
  61.9 60.3 %copy-start = (f32[256,1024]{1,0:T(8,128)}, f32[256,1024]{1,0:T(8,128)S(1)}, u32[]{:S(2)}) copy-start(f32[256,1024]{1,0:T(8,128)S(1)} %get-tuple-element.538) | copy-start | bytes 3145732
  62.6 4.1 %collective-permute-start.4 = (f32[4,1024]{1,0:T(4,128)S(1)}, f32[4,1024]{1,0:T(4,128)S(1)}, u32[]{:S(2)}, u32[]{:S(2)}) collective-permute-start(f32[4,1024]{1,0:T(4,128)S(1)} %slice.9), channel_id=1, source_target_pairs={{0,1},{1,2},{2,3},{3,4},{4,5},{5,6},{6,7},{7,0},{8,9},{9,10},{10,1... | collective-permute-start | bytes 49160 | tf_op jit(solution)/shard_map/ppermute | solution.py:11
  67.5 4.1 %collective-permute-start.5 = (f32[4,1024]{1,0:T(4,128)S(1)}, f32[4,1024]{1,0:T(4,128)S(1)}, u32[]{:S(2)}, u32[]{:S(2)}) collective-permute-start(f32[4,1024]{1,0:T(4,128)S(1)} %slice_add_fusion.1), channel_id=1, source_target_pairs={{0,1},{1,2},{2,3},{3,4},{4,5},{5,6},{6,7},{7,0},{8,9},{9,10},{10,1... | collective-permute-start | bytes 49160 | tf_op jit(solution)/shard_map/ppermute | solution.py:11
Sparse Core Ops, SparseCore 0:
  67.6 53.0 all-reduce.1
where the time goes:
time: 130 us; the launch traced here: 129 us
  waiting for transfers between devices  51.9 us (40%)
  blocking collectives  18 us (14%)
  between operations  14.1 us (11%)
  starting transfers between devices  14 us (11%)
  other arithmetic  12.9 us (10%)
  matrix products  9.27 us (7%)
  local copies, waits for them, and re-layouts  8.68 us (7%)
    psum x1, waiting for transfers between devices, shards(): grad_texts = lax.psum(grad_local_text, 'aud')  30.4 us
    ppermute x12, waiting for transfers between devices, from_behind(): lax.ppermute(shard, axis, [(i, (i + by) % size) for i in range(size)])  21.5 us
    psum x1, blocking collectives, shards(): grad_audio = lax.psum(returned, 'txt')  18 us
    ppermute x12, starting transfers between devices, from_behind(): lax.ppermute(shard, axis, [(i, (i + by) % size) for i in range(size)])  13.9 us
    dot_general x4, matrix products, block_terms(): lax.dot_general(image_half, products, (((1,), (1,)), ((), ())), preferred...  6.63 us
    add x4, other arithmetic, advance(): grad_window + more_window  5.11 us
    while x20, local copies, waits for them, and re-layouts  3.58 us
    add x4, other arithmetic, advance(): held_grad + more_piece  3.4 us
  transfers between devices with their start and end apart: 13, of which 10 were waited for; matrix products, arithmetic and copies ran while one was open for 17% of the time, Pallas kernels for 0%

commit v1 on v0

v1 whole, which is shorter than its diff:
```python
import functools
import jax
import jax.numpy as jnp
from jax import lax
from jax.experimental import pallas as pl
from jax.experimental.pallas import tpu as pltpu
from jax.sharding import PartitionSpec as P

HOPS = 2
MESH = pl.DeviceIdType.MESH
LANES = 128


def each(count, body, start=0):
    if count - start <= 8:
        for i in range(start, count):
            body(i)
    else:
        lax.fori_loop(start, count, lambda i, c: (body(i), c)[1], 0)


def kernel(
    n_txt,
    n_aud,
    images,
    texts,
    audio,
    pos_text,
    pos_audio,
    scale,
    bias,
    grad_images,
    grad_texts,
    grad_audio,
    image_buf,
    image_half,
    text_all,
    window,
    products,
    slopes,
    window_acc,
    text_out,
    text_in,
    text_sum,
    text_z,
    piece,
    pieces,
    home_out,
    home_in,
    audio_sum,
    audio_z,
    result_buf,
    load_sem,
    gather_send,
    gather_recv,
    relay_send,
    relay_recv,
    audio_send,
    audio_recv,
    scatter_send,
    scatter_recv,
    home_send,
    home_recv,
    z_send,
    z_recv,
    za_send,
    za_recv,
    spread_send,
    spread_recv,
    store_sem,
):
    t = lax.axis_index("txt")
    a = lax.axis_index("aud")
    text_rows, width = texts.shape
    half_rows = text_rows // 2
    block = audio.shape[0]
    slots = (HOPS + 1) * block
    cols = slots * text_rows
    chunk_rows, chunk_cols = piece.shape
    n_col = width // chunk_cols
    half = lax.rem(a, 2)
    other = 1 - half
    partner = a + 1 - 2 * half

    load_images = pltpu.make_async_copy(images, image_buf, load_sem.at[0])
    load_images.start()
    load_low = pltpu.make_async_copy(
        texts.at[pl.ds(0, half_rows)], text_all.at[t, 0], load_sem.at[1]
    )
    load_low.start()
    load_high = pltpu.make_async_copy(
        texts.at[pl.ds(half_rows, half_rows)], text_all.at[t, 1], load_sem.at[2]
    )
    load_high.start()
    load_audio = pltpu.make_async_copy(audio, window.at[0], load_sem.at[3])
    load_audio.start()

    barrier = pltpu.get_barrier_semaphore()

    def greet_plane(e):
        pl.semaphore_signal(
            barrier, inc=1, device_id=(t, lax.rem(a + e, n_aud)), device_id_type=MESH
        )

    def greet_line(d):
        pl.semaphore_signal(
            barrier, inc=1, device_id=(lax.rem(t + d, n_txt), a), device_id_type=MESH
        )

    each(n_aud, greet_plane, 1)
    each(n_txt, greet_line, 1)
    pl.semaphore_wait(barrier, n_aud + n_txt - 2)

    def audio_copy(k):
        return pltpu.make_async_remote_copy(
            src_ref=audio,
            dst_ref=window.at[k],
            send_sem=audio_send.at[k],
            recv_sem=audio_recv.at[k],
            device_id=(t, lax.rem(a + n_aud - k, n_aud)),
            device_id_type=MESH,
        )

    def gather_copy(d):
        return pltpu.make_async_remote_copy(
            src_ref=texts.at[pl.ds(pl.multiple_of(half * half_rows, half_rows), half_rows)],
            dst_ref=text_all.at[t, half],
            send_sem=gather_send.at[d],
            recv_sem=gather_recv.at[d],
            device_id=(lax.rem(t + d, n_txt), a),
            device_id_type=MESH,
        )

    def relay_copy(d):
        source = lax.rem(t + n_txt - d, n_txt)
        return pltpu.make_async_remote_copy(
            src_ref=text_all.at[source, half],
            dst_ref=text_all.at[source, half],
            send_sem=relay_send.at[d],
            recv_sem=relay_recv.at[d],
            device_id=(t, partner),
            device_id_type=MESH,
        )

    for k in range(1, HOPS + 1):
        audio_copy(k).start()
    each(n_txt, lambda d: gather_copy(d).start(), 1)

    temper = scale[0]
    offset = bias[0]

    load_images.wait()
    image_half[...] = image_buf[...].astype(jnp.bfloat16)
    window_acc[...] = jnp.zeros_like(window_acc)
    load_low.wait()
    load_high.wait()
    load_audio.wait()
    for k in range(1, HOPS + 1):
        audio_copy(k).wait()

    tile = min(width, 256)

    def scatter_copy(s, e):
        peer = lax.rem(a + e, n_aud)
        return pltpu.make_async_remote_copy(
            src_ref=text_out.at[s, peer],
            dst_ref=text_in.at[e, s],
            send_sem=scatter_send,
            recv_sem=scatter_recv,
            device_id=(t, peer),
            device_id_type=MESH,
        )

    def process(d):
        s = lax.rem(t + n_txt - d, n_txt)
        base = d * cols if isinstance(d, int) else pl.multiple_of(d * cols, cols)
        held = text_all[s].reshape(text_rows, width)
        for w in range(slots):
            row = window[w // block, pl.ds(w % block, 1), :]
            products[pl.ds(base + w * text_rows, text_rows), :] = (held * row).astype(
                jnp.bfloat16
            )
        logits = (
            temper
            * lax.dot_general(
                products[pl.ds(base, cols), :],
                image_half[...],
                (((1,), (1,)), ((), ())),
                preferred_element_type=jnp.float32,
            )
            + offset
        )
        local = pos_text[...] - s * text_rows
        inside = (local >= 0) & (local < text_rows)
        target = jnp.where(inside, pos_audio[...] * text_rows + local, -1)
        index = lax.broadcasted_iota(jnp.int32, logits.shape, 0)
        positive = jnp.where(index == target, 1.0, 0.0)
        slope = ((jax.nn.sigmoid(logits) - positive) * temper).astype(jnp.bfloat16)
        slopes[pl.ds(base, cols), :] = slope
        for first in range(0, width, tile):
            grad = jnp.dot(
                slope, image_half[:, first : first + tile], preferred_element_type=jnp.float32
            )
            text_part = held[:, first : first + tile]
            total = jnp.zeros((text_rows, tile), jnp.float32)
            for w in range(slots):
                part = grad[w * text_rows : (w + 1) * text_rows]
                total = total + part * window[
                    w // block, pl.ds(w % block, 1), pl.ds(first, tile)
                ]
                weighted = part * text_part
                folded = weighted[0:8]
                for r in range(8, text_rows, 8):
                    folded = folded + weighted[r : r + 8]
                window_acc[w, :, pl.ds(first, tile)] += folded
            for c in range(first // chunk_cols, (first + tile) // chunk_cols):
                for r in range(text_rows // chunk_rows):
                    text_out[s, r * n_col + c] = total[
                        r * chunk_rows : (r + 1) * chunk_rows,
                        c * chunk_cols - first : (c + 1) * chunk_cols - first,
                    ]
        each(n_aud, lambda e: scatter_copy(s, e).start(), 1)

    process(0)

    def pass_on(d):
        gather_copy(d).wait()
        relay_copy(d).start()

    each(n_txt, pass_on, 1)

    def next_block(d, carry):
        relay_copy(d).wait()
        process(d)
        return carry

    lax.fori_loop(1, n_txt, next_block, 0)

    for w in range(slots):
        home_out[w // block, pl.ds(w % block, 1), :] = jnp.sum(
            window_acc[w], axis=0, keepdims=True
        )

    def home_copy(k):
        return pltpu.make_async_remote_copy(
            src_ref=home_out.at[k],
            dst_ref=home_in.at[k],
            send_sem=home_send.at[k],
            recv_sem=home_recv.at[k],
            device_id=(t, lax.rem(a + k, n_aud)),
            device_id_type=MESH,
        )

    for k in range(1, HOPS + 1):
        home_copy(k).start()

    stores = []
    for number, first in enumerate(range(0, width, tile)):
        result_buf[:, first : first + tile] = lax.dot_general(
            slopes[...],
            products[:, first : first + tile],
            (((0,), (0,)), ((), ())),
            preferred_element_type=jnp.float32,
        )
        store = pltpu.make_async_copy(
            result_buf.at[:, pl.ds(first, tile)],
            grad_images.at[:, pl.ds(first, tile)],
            store_sem.at[number],
        )
        store.start()
        stores.append(store)

    arrived = text_in.at[pl.ds(1, n_aud - 1)]
    gathered = pltpu.make_async_remote_copy(
        src_ref=arrived,
        dst_ref=arrived,
        send_sem=scatter_send,
        recv_sem=scatter_recv,
        device_id=(t, partner),
        device_id_type=MESH,
    )
    gathered.wait_recv()
    for s in range(n_txt):
        total = text_out[s, a]
        for e in range(1, n_aud):
            total = total + text_in[e, s]
        text_sum[s] = total

    def z_copy(d):
        to = lax.rem(t + d, n_txt)
        return pltpu.make_async_remote_copy(
            src_ref=text_sum.at[to],
            dst_ref=text_z.at[t],
            send_sem=z_send.at[d],
            recv_sem=z_recv.at[d],
            device_id=(to, a),
            device_id_type=MESH,
        )

    def za_copy(d):
        return pltpu.make_async_remote_copy(
            src_ref=audio_sum,
            dst_ref=audio_z.at[t],
            send_sem=za_send.at[d],
            recv_sem=za_recv.at[d],
            device_id=(lax.rem(t + d, n_txt), a),
            device_id_type=MESH,
        )

    each(n_txt, lambda d: z_copy(d).start(), 1)
    text_z[t] = text_sum[t]

    total = home_out[0]
    for k in range(1, HOPS + 1):
        home_copy(k).wait()
        total = total + home_in[k]
    audio_sum[...] = total
    audio_z[t] = total
    each(n_txt, lambda d: za_copy(d).start(), 1)

    each(n_txt, lambda d: z_copy(d).wait(), 1)
    total = text_z[0]
    for s in range(1, n_txt):
        total = total + text_z[s]
    piece[...] = total
    pieces[a] = total

    def spread_copy(e):
        return pltpu.make_async_remote_copy(
            src_ref=piece,
            dst_ref=pieces.at[a],
            send_sem=spread_send.at[e],
            recv_sem=spread_recv.at[e],
            device_id=(t, lax.rem(a + e, n_aud)),
            device_id_type=MESH,
        )

    each(n_aud, lambda e: spread_copy(e).start(), 1)

    each(n_txt, lambda d: za_copy(d).wait(), 1)
    total = audio_z[0]
    for s in range(1, n_txt):
        total = total + audio_z[s]
    grad_audio[...] = total

    each(n_aud, lambda e: spread_copy(e).wait(), 1)
    for c in range(n_col):
        for r in range(text_rows // chunk_rows):
            grad_texts[
                r * chunk_rows : (r + 1) * chunk_rows, c * chunk_cols : (c + 1) * chunk_cols
            ] = pieces[r * n_col + c]

    gathered.wait_send()
    for store in stores:
        store.wait()


def shards(n_txt, n_aud, images, texts, audio, pos_text, pos_audio, logit_scale, logit_bias):
    rows, width = images.shape
    text_rows = texts.shape[0]
    block = audio.shape[0]
    slots = (HOPS + 1) * block
    cols = slots * text_rows
    n_col = min(n_aud, width // LANES)
    n_row = n_aud // n_col
    chunk = (text_rows // n_row, width // n_col)
    f32, bf16 = jnp.float32, jnp.bfloat16
    vmem = pl.BlockSpec(memory_space=pltpu.VMEM)
    smem = pl.BlockSpec(memory_space=pltpu.SMEM)
    anywhere = pl.BlockSpec(memory_space=pl.ANY)
    dma = pltpu.SemaphoreType.DMA
    return pl.pallas_call(
        functools.partial(kernel, n_txt, n_aud),
        out_shape=(
            jax.ShapeDtypeStruct((rows, width), f32),
            jax.ShapeDtypeStruct((text_rows, width), f32),
            jax.ShapeDtypeStruct((block, width), f32),
        ),
        in_specs=[anywhere, anywhere, anywhere, vmem, vmem, smem, smem],
        out_specs=(anywhere, vmem, vmem),
        scratch_shapes=[
            pltpu.VMEM((rows, width), f32),
            pltpu.VMEM((rows, width), bf16),
            pltpu.VMEM((n_txt, 2, text_rows // 2, width), f32),
            pltpu.VMEM((HOPS + 1, block, width), f32),
            pltpu.VMEM((n_txt * cols, width), bf16),
            pltpu.VMEM((n_txt * cols, rows), bf16),
            pltpu.VMEM((slots, 8, width), f32),
            pltpu.VMEM((n_txt, n_aud) + chunk, f32),
            pltpu.VMEM((n_aud, n_txt) + chunk, f32),
            pltpu.VMEM((n_txt,) + chunk, f32),
            pltpu.VMEM((n_txt,) + chunk, f32),
            pltpu.VMEM(chunk, f32),
            pltpu.VMEM((n_aud,) + chunk, f32),
            pltpu.VMEM((HOPS + 1, block, width), f32),
            pltpu.VMEM((HOPS + 1, block, width), f32),
            pltpu.VMEM((block, width), f32),
            pltpu.VMEM((n_txt, block, width), f32),
            pltpu.VMEM((rows, width), f32),
            dma((4,)),
            dma((n_txt,)),
            dma((n_txt,)),
            dma((n_txt,)),
            dma((n_txt,)),
            dma((HOPS + 1,)),
            dma((HOPS + 1,)),
            dma,
            dma,
            dma((HOPS + 1,)),
            dma((HOPS + 1,)),
            dma((n_txt,)),
            dma((n_txt,)),
            dma((n_txt,)),
            dma((n_txt,)),
            dma((n_aud,)),
            dma((n_aud,)),
            dma((max(1, width // 256),)),
        ],
        compiler_params=pltpu.CompilerParams(
            collective_id=0, has_side_effects=True, vmem_limit_bytes=56 * 1024 * 1024
        ),
        name="trilinear",
    )(
        images,
        texts,
        audio,
        pos_text.reshape(1, rows),
        pos_audio.reshape(1, rows),
        logit_scale,
        logit_bias,
    )


def solution(mesh):
    placed = (
        P(("txt", "aud"), None),
        P("txt", None),
        P("aud", None),
        P(("txt", "aud")),
        P(("txt", "aud")),
        P(),
        P(),
    )
    return jax.shard_map(
        functools.partial(shards, mesh.shape["txt"], mesh.shape["aud"]),
        mesh=mesh,
        in_specs=placed,
        out_specs=(P(("txt", "aud"), None), P("txt", None), P("aud", None)),
        check_vma=False,
    )
```

time: 130 us -> 30.7 us (0.24)
  waiting for transfers between devices: 51.9 us -> 0 us
  Pallas kernels: 0 us -> 24.8 us
  blocking collectives: 18 us -> 0 us
  starting transfers between devices: 14 us -> 0 us
  other arithmetic: 12.9 us -> 0 us
  between operations: 14.1 us -> 1.94 us
  matrix products: 9.27 us -> 0 us
  local copies, waits for them, and re-layouts: 8.68 us -> 3.66 us
    psum x1 -> x0, waiting for transfers between devices: 30.4 us -> none  [shards(): grad_texts = lax.psum(grad_local_text, 'aud')]
    pallas_call x0 -> x1, Pallas kernels: none -> 24.8 us  [shards(): pl.pallas_call(functools.partial(kernel, n_txt, n_aud), out_shape=(jax.Sh...]
    ppermute x12 -> x0, waiting for transfers between devices: 21.5 us -> none  [from_behind(): lax.ppermute(shard, axis, [(i, (i + by) % size) for i in range(size)])]
    psum x1 -> x0, blocking collectives: 18 us -> none  [shards(): grad_audio = lax.psum(returned, 'txt')]
    ppermute x12 -> x0, starting transfers between devices: 13.9 us -> none  [from_behind(): lax.ppermute(shard, axis, [(i, (i + by) % size) for i in range(size)])]
    add x10 -> x0, other arithmetic: 10 us -> none  [the longest x4 5.11 us: advance(): grad_window + more_window]
    dot_general x12 -> x0, matrix products: 9.27 us -> none  [the longest x4 6.63 us: block_terms(): lax.dot_general(image_half, products, (((1,), (1,)), ((), ())), preferred...]
    while x20 -> x0, local copies, waits for them, and re-layouts: 3.58 us -> none
  transfers between devices with their start and end apart: 13 -> 0, of which waited for: 10 -> 0; matrix products, arithmetic and copies ran while one was open for 17% -> 0% of each run, Pallas kernels for 0% -> 0%
where the time goes in v1:
time: 30.7 us; the launch traced here: 30.4 us
  Pallas kernels  24.8 us (81%)
  local copies, waits for them, and re-layouts  3.66 us (12%)
  between operations  1.94 us (6%)
    pallas_call x1, Pallas kernels, shards(): pl.pallas_call(functools.partial(kernel, n_txt, n_aud), out_shape=(jax.Sh...  24.8 us
    unnamed x7, local copies, waits for them, and re-layouts  3.66 us

profile of v1, /device:TPU:0, one launch (start us, length us, event | category | flops | bytes accessed | tf_op | source)
XLA Modules:
  0.0 30.4 jit_solution(1064651720834321209)
XLA Ops:
  1.9 24.8 %trilinear.1 = (f32[256,1024]{1,0:T(8,128)}, f32[16,1024]{1,0:T(8,128)}, f32[4,1024]{1,0:T(4,128)}) custom-call(f32[256,1024]{1,0:T(8,128)} %images.1, f32[16,1024]{1,0:T(8,128)} %texts.1, f32[4,1024]{1,0:T(4,128)} %audio.1, s32[1,256]{1,0:T(1,128)} %bitcast.2, s32[1,256]{1,0:T(1,128)} %bitcast.3, f32[1]{0:T(128)S(6)} %copy.13.scale, f32[1]{0:T(128)S(6)} %copy.14.bias), custom_call_target="tpu_custom_call" | custom-call | tf_op jit(solution)/shard_map/trilinear/pallas_call | solution.py:372
  26.7 0.0 copy-start
  26.7 2.3 %copy.15 = f32[256,1024]{1,0:T(8,128)} copy(f32[256,1024]{1,0:T(8,128)} %get-tuple-element.6) | data formatting | bytes 2097152
  29.1 0.0 copy-done
  29.1 0.0 copy-start.1
  29.1 0.6 %copy.16 = f32[16,1024]{1,0:T(8,128)} copy(f32[16,1024]{1,0:T(8,128)S(1)} %copy-done) | data formatting | bytes 131072
  29.7 0.1 copy-done.1
  29.8 0.6 %copy.17 = f32[4,1024]{1,0:T(4,128)} copy(f32[4,1024]{1,0:T(4,128)S(1)} %copy-done.1) | data formatting | bytes 32768
Async XLA Ops:
  26.7 2.4 %copy-start = (f32[16,1024]{1,0:T(8,128)S(1)}, f32[16,1024]{1,0:T(8,128)}, u32[]{:S(2)}) copy-start(f32[16,1024]{1,0:T(8,128)} %get-tuple-element.7) | copy-start | bytes 196612
  29.1 0.7 %copy-start.1 = (f32[4,1024]{1,0:T(4,128)S(1)}, f32[4,1024]{1,0:T(4,128)}, u32[]{:S(2)}) copy-start(f32[4,1024]{1,0:T(4,128)} %get-tuple-element.8) | copy-start | bytes 49156

commit v2 on v1

--- a/solution.py
+++ b/solution.py
@@ -19,19 +19,32 @@
         lax.fori_loop(start, count, lambda i, c: (body(i), c)[1], 0)
 
 
+def each_far_first(count, place, body):
+    above = count - 1 - place
+
+    def step(i):
+        body(jnp.where(i < above, above - i, i + 1))
+
+    each(count - 1, step)
+
+
 def kernel(
     n_txt,
     n_aud,
     images,
     texts,
     audio,
+    pos_text_in,
+    pos_audio_in,
+    scale_in,
+    bias_in,
+    grad_images,
+    grad_texts,
+    grad_audio,
     pos_text,
     pos_audio,
     scale,
     bias,
-    grad_images,
-    grad_texts,
-    grad_audio,
     image_buf,
     image_half,
     text_all,
@@ -49,7 +62,6 @@
     home_in,
     audio_sum,
     audio_z,
-    result_buf,
     load_sem,
     gather_send,
     gather_recv,
@@ -67,7 +79,6 @@
     za_recv,
     spread_send,
     spread_recv,
-    store_sem,
 ):
     t = lax.axis_index("txt")
     a = lax.axis_index("aud")
@@ -82,8 +93,21 @@
     other = 1 - half
     partner = a + 1 - 2 * half
 
-    load_images = pltpu.make_async_copy(images, image_buf, load_sem.at[0])
-    load_images.start()
+    barrier = pltpu.get_barrier_semaphore()
+
+    def greet_plane(e):
+        pl.semaphore_signal(
+            barrier, inc=1, device_id=(t, lax.rem(a + e, n_aud)), device_id_type=MESH
+        )
+
+    def greet_line(d):
+        pl.semaphore_signal(
+            barrier, inc=1, device_id=(lax.rem(t + d, n_txt), a), device_id_type=MESH
+        )
+
+    each(n_txt, greet_line, 1)
+    each(n_aud, greet_plane, 1)
+
     load_low = pltpu.make_async_copy(
         texts.at[pl.ds(0, half_rows)], text_all.at[t, 0], load_sem.at[1]
     )
@@ -94,26 +118,29 @@
     load_high.start()
     load_audio = pltpu.make_async_copy(audio, window.at[0], load_sem.at[3])
     load_audio.start()
-
-    barrier = pltpu.get_barrier_semaphore()
-
-    def greet_plane(e):
-        pl.semaphore_signal(
-            barrier, inc=1, device_id=(t, lax.rem(a + e, n_aud)), device_id_type=MESH
-        )
-
-    def greet_line(d):
-        pl.semaphore_signal(
-            barrier, inc=1, device_id=(lax.rem(t + d, n_txt), a), device_id_type=MESH
-        )
-
-    each(n_aud, greet_plane, 1)
-    each(n_txt, greet_line, 1)
+    load_images = pltpu.make_async_copy(images, image_buf, load_sem.at[0])
+    load_images.start()
+    small = [
+        pltpu.make_async_copy(src, dst, load_sem.at[4 + i])
+        for i, (src, dst) in enumerate(
+            (
+                (pos_text_in, pos_text),
+                (pos_audio_in, pos_audio),
+                (scale_in, scale),
+                (bias_in, bias),
+            )
+        )
+    ]
+    for load in small:
+        load.start()
+    load_low.wait()
+    load_high.wait()
+    load_audio.wait()
     pl.semaphore_wait(barrier, n_aud + n_txt - 2)
 
     def audio_copy(k):
         return pltpu.make_async_remote_copy(
-            src_ref=audio,
+            src_ref=window.at[0],
             dst_ref=window.at[k],
             send_sem=audio_send.at[k],
             recv_sem=audio_recv.at[k],
@@ -123,7 +150,7 @@
 
     def gather_copy(d):
         return pltpu.make_async_remote_copy(
-            src_ref=texts.at[pl.ds(pl.multiple_of(half * half_rows, half_rows), half_rows)],
+            src_ref=text_all.at[t, half],
             dst_ref=text_all.at[t, half],
             send_sem=gather_send.at[d],
             recv_sem=gather_recv.at[d],
@@ -144,17 +171,16 @@
 
     for k in range(1, HOPS + 1):
         audio_copy(k).start()
-    each(n_txt, lambda d: gather_copy(d).start(), 1)
-
+    each_far_first(n_txt, t, lambda d: gather_copy(d).start())
+
+    for load in small:
+        load.wait()
     temper = scale[0]
     offset = bias[0]
 
     load_images.wait()
     image_half[...] = image_buf[...].astype(jnp.bfloat16)
     window_acc[...] = jnp.zeros_like(window_acc)
-    load_low.wait()
-    load_high.wait()
-    load_audio.wait()
     for k in range(1, HOPS + 1):
         audio_copy(k).wait()
 
@@ -254,21 +280,13 @@
     for k in range(1, HOPS + 1):
         home_copy(k).start()
 
-    stores = []
-    for number, first in enumerate(range(0, width, tile)):
-        result_buf[:, first : first + tile] = lax.dot_general(
+    for first in range(0, width, tile):
+        grad_images[:, first : first + tile] = lax.dot_general(
             slopes[...],
             products[:, first : first + tile],
             (((0,), (0,)), ((), ())),
             preferred_element_type=jnp.float32,
         )
-        store = pltpu.make_async_copy(
-            result_buf.at[:, pl.ds(first, tile)],
-            grad_images.at[:, pl.ds(first, tile)],
-            store_sem.at[number],
-        )
-        store.start()
-        stores.append(store)
 
     arrived = text_in.at[pl.ds(1, n_aud - 1)]
     gathered = pltpu.make_async_remote_copy(
@@ -307,7 +325,7 @@
             device_id_type=MESH,
         )
 
-    each(n_txt, lambda d: z_copy(d).start(), 1)
+    each_far_first(n_txt, t, lambda d: z_copy(d).start())
     text_z[t] = text_sum[t]
 
     total = home_out[0]
@@ -316,7 +334,7 @@
         total = total + home_in[k]
     audio_sum[...] = total
     audio_z[t] = total
-    each(n_txt, lambda d: za_copy(d).start(), 1)
+    each_far_first(n_txt, t, lambda d: za_copy(d).start())
 
     each(n_txt, lambda d: z_copy(d).wait(), 1)
     total = text_z[0]
@@ -351,8 +369,18 @@
             ] = pieces[r * n_col + c]
 
     gathered.wait_send()
-    for store in stores:
-        store.wait()
+
+
+def put_out(*refs):
+    count = len(refs) // 2
+    sems = refs[-1]
+    copies = [
+        pltpu.make_async_copy(refs[i], refs[count + i], sems.at[i]) for i in range(count)
+    ]
+    for copy in copies:
+        copy.start()
+    for copy in copies:
+        copy.wait()
 
 
 def shards(n_txt, n_aud, images, texts, audio, pos_text, pos_audio, logit_scale, logit_bias):
@@ -366,19 +394,19 @@
     chunk = (text_rows // n_row, width // n_col)
     f32, bf16 = jnp.float32, jnp.bfloat16
     vmem = pl.BlockSpec(memory_space=pltpu.VMEM)
-    smem = pl.BlockSpec(memory_space=pltpu.SMEM)
-    anywhere = pl.BlockSpec(memory_space=pl.ANY)
+    anywhere = pl.BlockSpec(memory_space=pltpu.HBM)
     dma = pltpu.SemaphoreType.DMA
-    return pl.pallas_call(
+    shapes = ((rows, width), (text_rows, width), (block, width))
+    held = pl.pallas_call(
         functools.partial(kernel, n_txt, n_aud),
-        out_shape=(
-            jax.ShapeDtypeStruct((rows, width), f32),
-            jax.ShapeDtypeStruct((text_rows, width), f32),
-            jax.ShapeDtypeStruct((block, width), f32),
-        ),
-        in_specs=[anywhere, anywhere, anywhere, vmem, vmem, smem, smem],
-        out_specs=(anywhere, vmem, vmem),
+        out_shape=tuple(pltpu.VMEM(shape, f32) for shape in shapes),
+        in_specs=[anywhere] * 7,
+        out_specs=(vmem,) * 3,
         scratch_shapes=[
+            pltpu.VMEM((1, rows), jnp.int32),
+            pltpu.VMEM((1, rows), jnp.int32),
+            pltpu.SMEM((1,), f32),
+            pltpu.SMEM((1,), f32),
             pltpu.VMEM((rows, width), f32),
             pltpu.VMEM((rows, width), bf16),
             pltpu.VMEM((n_txt, 2, text_rows // 2, width), f32),
@@ -396,8 +424,7 @@
             pltpu.VMEM((HOPS + 1, block, width), f32),
             pltpu.VMEM((block, width), f32),
             pltpu.VMEM((n_txt, block, width), f32),
-            pltpu.VMEM((rows, width), f32),
-            dma((4,)),
+            dma((8,)),
             dma((n_txt,)),
             dma((n_txt,)),
             dma((n_txt,)),
@@ -414,7 +441,6 @@
             dma((n_txt,)),
             dma((n_aud,)),
             dma((n_aud,)),
-            dma((max(1, width // 256),)),
         ],
         compiler_params=pltpu.CompilerParams(
             collective_id=0, has_side_effects=True, vmem_limit_bytes=56 * 1024 * 1024
@@ -429,6 +455,14 @@
         logit_scale,
         logit_bias,
     )
+    return pl.pallas_call(
+        put_out,
+        out_shape=tuple(jax.ShapeDtypeStruct(shape, f32) for shape in shapes),
+        in_specs=[vmem] * 3,
+        out_specs=(anywhere,) * 3,
+        scratch_shapes=[dma((3,))],
+        name="put_out",
+    )(*[pltpu.with_memory_space_constraint(h, pltpu.VMEM) for h in held])
 
 
 def solution(mesh):

time: 30.7 us -> 26.5 us (0.86)
  local copies, waits for them, and re-layouts: 3.66 us -> 0 us
  Pallas kernels: 24.8 us -> 24.4 us
    unnamed x7 -> x0, local copies, waits for them, and re-layouts: 3.66 us -> none
    pallas_call x1 -> x2, Pallas kernels: 24.8 us -> 24.4 us  [the longest x1 23.4 us: shards(): pl.pallas_call(functools.partial(kernel, n_txt, n_aud), out_shape=tuple((...]
where the time goes in v2:
time: 26.5 us; the launch traced here: 26.3 us
  Pallas kernels  24.4 us (92%)
  between operations  1.93 us (7%)
    pallas_call x1, Pallas kernels, shards(): pl.pallas_call(functools.partial(kernel, n_txt, n_aud), out_shape=tuple((...  23.4 us
    pallas_call x1, Pallas kernels, shards(): pl.pallas_call(put_out, out_shape=tuple((jax.ShapeDtypeStruct(shape, f32)...  1.01 us

profile of v2, /device:TPU:0, one launch (start us, length us, event | category | flops | bytes accessed | tf_op | source)
XLA Modules:
  0.0 26.3 jit_solution(17318433552939697370)
XLA Ops:
  1.9 23.4 %trilinear.1 = (f32[256,1024]{1,0:T(8,128)S(1)}, f32[16,1024]{1,0:T(8,128)S(1)}, f32[4,1024]{1,0:T(4,128)S(1)}) custom-call(f32[256,1024]{1,0:T(8,128)} %images.1, f32[16,1024]{1,0:T(8,128)} %texts.1, f32[4,1024]{1,0:T(4,128)} %audio.1, s32[1,256]{1,0:T(1,128)} %bitcast.2, s32[1,256]{1,0:T(1,128)} %bitcast.3, f32[1]{0:T(128)S(6)} %copy.10.scale_in, ...), custom_call_target="tpu_custom_call" | custom-call | tf_op jit(solution)/shard_map/trilinear/pallas_call | solution.py:400
  25.3 1.0 %put_out.1 = (f32[256,1024]{1,0:T(8,128)}, f32[16,1024]{1,0:T(8,128)}, f32[4,1024]{1,0:T(4,128)}) custom-call(f32[256,1024]{1,0:T(8,128)S(1)} %get-tuple-element.6.refs_0_, f32[16,1024]{1,0:T(8,128)S(1)} %get-tuple-element.7.refs_1_, f32[4,1024]{1,0:T(4,128)S(1)} %get-tuple-element.8.refs_2_), custom_call_target="tpu_custom_call" | custom-call | tf_op jit(solution)/shard_map/put_out/pallas_call | solution.py:458

commit v3 on v2

--- a/solution.py
+++ b/solution.py
@@ -90,7 +90,6 @@
     chunk_rows, chunk_cols = piece.shape
     n_col = width // chunk_cols
     half = lax.rem(a, 2)
-    other = 1 - half
     partner = a + 1 - 2 * half
 
     barrier = pltpu.get_barrier_semaphore()
@@ -186,20 +185,25 @@
 
     tile = min(width, 256)
 
-    def scatter_copy(s, e):
+    def scatter_copy(turn, s, e):
         peer = lax.rem(a + e, n_aud)
         return pltpu.make_async_remote_copy(
             src_ref=text_out.at[s, peer],
-            dst_ref=text_in.at[e, s],
+            dst_ref=text_in.at[s, e],
             send_sem=scatter_send,
-            recv_sem=scatter_recv,
+            recv_sem=scatter_recv.at[turn],
             device_id=(t, peer),
             device_id_type=MESH,
         )
 
-    def process(d):
+    def owner(turn):
+        low_first = jnp.where(turn <= t, t + 1 - turn, turn)
+        high_first = jnp.where(turn < n_txt - t, t + turn, n_txt - turn)
+        return jnp.where(2 * t >= n_txt, low_first, high_first)
+
+    def process(turn, d):
         s = lax.rem(t + n_txt - d, n_txt)
-        base = d * cols if isinstance(d, int) else pl.multiple_of(d * cols, cols)
+        base = turn * cols if isinstance(turn, int) else pl.multiple_of(turn * cols, cols)
         held = text_all[s].reshape(text_rows, width)
         for w in range(slots):
             row = window[w // block, pl.ds(w % block, 1), :]
@@ -245,19 +249,21 @@
                         r * chunk_rows : (r + 1) * chunk_rows,
                         c * chunk_cols - first : (c + 1) * chunk_cols - first,
                     ]
-        each(n_aud, lambda e: scatter_copy(s, e).start(), 1)
-
-    process(0)
-
-    def pass_on(d):
+        each(n_aud, lambda e: scatter_copy(turn, s, e).start(), 1)
+
+    process(0, 0)
+
+    def pass_on(turn):
+        d = owner(turn)
         gather_copy(d).wait()
         relay_copy(d).start()
 
     each(n_txt, pass_on, 1)
 
-    def next_block(d, carry):
+    def next_block(turn, carry):
+        d = owner(turn)
         relay_copy(d).wait()
-        process(d)
+        process(turn, d)
         return carry
 
     lax.fori_loop(1, n_txt, next_block, 0)
@@ -288,21 +294,20 @@
             preferred_element_type=jnp.float32,
         )
 
-    arrived = text_in.at[pl.ds(1, n_aud - 1)]
-    gathered = pltpu.make_async_remote_copy(
-        src_ref=arrived,
-        dst_ref=arrived,
-        send_sem=scatter_send,
-        recv_sem=scatter_recv,
-        device_id=(t, partner),
-        device_id_type=MESH,
-    )
-    gathered.wait_recv()
-    for s in range(n_txt):
+    def reduced(turn, s):
+        arrived = text_in.at[s, pl.ds(1, n_aud - 1)]
+        pltpu.make_async_remote_copy(
+            src_ref=arrived,
+            dst_ref=arrived,
+            send_sem=scatter_send,
+            recv_sem=scatter_recv.at[turn],
+            device_id=(t, partner),
+            device_id_type=MESH,
+        ).wait_recv()
         total = text_out[s, a]
         for e in range(1, n_aud):
-            total = total + text_in[e, s]
-        text_sum[s] = total
+            total = total + text_in[s, e]
+        return total
 
     def z_copy(d):
         to = lax.rem(t + d, n_txt)
@@ -325,8 +330,13 @@
             device_id_type=MESH,
         )
 
-    each_far_first(n_txt, t, lambda d: z_copy(d).start())
-    text_z[t] = text_sum[t]
+    def send_back(turn):
+        d = owner(turn)
+        s = lax.rem(t + n_txt - d, n_txt)
+        text_sum[s] = reduced(turn, s)
+        z_copy(n_txt - d).start()
+
+    each(n_txt - 1, send_back, 1)
 
     total = home_out[0]
     for k in range(1, HOPS + 1):
@@ -336,6 +346,8 @@
     audio_z[t] = total
     each_far_first(n_txt, t, lambda d: za_copy(d).start())
 
+    send_back(n_txt - 1)
+    text_z[t] = reduced(0, t)
     each(n_txt, lambda d: z_copy(d).wait(), 1)
     total = text_z[0]
     for s in range(1, n_txt):
@@ -368,7 +380,15 @@
                 r * chunk_rows : (r + 1) * chunk_rows, c * chunk_cols : (c + 1) * chunk_cols
             ] = pieces[r * n_col + c]
 
-    gathered.wait_send()
+    sent = text_in.at[:, pl.ds(1, n_aud - 1)]
+    pltpu.make_async_remote_copy(
+        src_ref=sent,
+        dst_ref=sent,
+        send_sem=scatter_send,
+        recv_sem=scatter_recv.at[0],
+        device_id=(t, partner),
+        device_id_type=MESH,
+    ).wait_send()
 
 
 def put_out(*refs):
@@ -415,7 +435,7 @@
             pltpu.VMEM((n_txt * cols, rows), bf16),
             pltpu.VMEM((slots, 8, width), f32),
             pltpu.VMEM((n_txt, n_aud) + chunk, f32),
-            pltpu.VMEM((n_aud, n_txt) + chunk, f32),
+            pltpu.VMEM((n_txt, n_aud) + chunk, f32),
             pltpu.VMEM((n_txt,) + chunk, f32),
             pltpu.VMEM((n_txt,) + chunk, f32),
             pltpu.VMEM(chunk, f32),
@@ -432,7 +452,7 @@
             dma((HOPS + 1,)),
             dma((HOPS + 1,)),
             dma,
-            dma,
+            dma((n_txt,)),
             dma((HOPS + 1,)),
             dma((HOPS + 1,)),
             dma((n_txt,)),

time: 26.5 us -> 26.2 us (0.989)
  Pallas kernels: 24.4 us -> 24.1 us
    pallas_call x1, Pallas kernels: 23.4 us -> 23.1 us  [shards(): pl.pallas_call(functools.partial(kernel, n_txt, n_aud), out_shape=tuple((...]
where the time goes in v3:
time: 26.2 us; the launch traced here: 26 us
  Pallas kernels  24.1 us (92%)
  between operations  1.93 us (7%)
    pallas_call x1, Pallas kernels, shards(): pl.pallas_call(functools.partial(kernel, n_txt, n_aud), out_shape=tuple((...  23.1 us
    pallas_call x1, Pallas kernels, shards(): pl.pallas_call(put_out, out_shape=tuple((jax.ShapeDtypeStruct(shape, f32)...  1.01 us

profile of v3, /device:TPU:0, one launch (start us, length us, event | category | flops | bytes accessed | tf_op | source)
XLA Modules:
  0.0 26.0 jit_solution(9897952533043898052)
XLA Ops:
  1.9 23.1 %trilinear.1 = (f32[256,1024]{1,0:T(8,128)S(1)}, f32[16,1024]{1,0:T(8,128)S(1)}, f32[4,1024]{1,0:T(4,128)S(1)}) custom-call(f32[256,1024]{1,0:T(8,128)} %images.1, f32[16,1024]{1,0:T(8,128)} %texts.1, f32[4,1024]{1,0:T(4,128)} %audio.1, s32[1,256]{1,0:T(1,128)} %bitcast.2, s32[1,256]{1,0:T(1,128)} %bitcast.3, f32[1]{0:T(128)S(6)} %copy.10.scale_in, ...), custom_call_target="tpu_custom_call" | custom-call | tf_op jit(solution)/shard_map/trilinear/pallas_call | solution.py:420
  25.0 1.0 %put_out.1 = (f32[256,1024]{1,0:T(8,128)}, f32[16,1024]{1,0:T(8,128)}, f32[4,1024]{1,0:T(4,128)}) custom-call(f32[256,1024]{1,0:T(8,128)S(1)} %get-tuple-element.6.refs_0_, f32[16,1024]{1,0:T(8,128)S(1)} %get-tuple-element.7.refs_1_, f32[4,1024]{1,0:T(4,128)S(1)} %get-tuple-element.8.refs_2_), custom_call_target="tpu_custom_call" | custom-call | tf_op jit(solution)/shard_map/put_out/pallas_call | solution.py:478

commit v4 on v3

--- a/solution.py
+++ b/solution.py
@@ -251,14 +251,13 @@
                     ]
         each(n_aud, lambda e: scatter_copy(turn, s, e).start(), 1)
 
-    process(0, 0)
-
     def pass_on(turn):
         d = owner(turn)
         gather_copy(d).wait()
         relay_copy(d).start()
 
     each(n_txt, pass_on, 1)
+    process(0, 0)
 
     def next_block(turn, carry):
         d = owner(turn)

time: 26.2 us -> 26.2 us (level)
  no operation moved by 1% of the time
where the time goes in v4:
time: 26.2 us; the launch traced here: 26.1 us
  Pallas kernels  24.1 us (92%)
  between operations  1.93 us (7%)
    pallas_call x1, Pallas kernels, shards(): pl.pallas_call(functools.partial(kernel, n_txt, n_aud), out_shape=tuple((...  23.1 us
    pallas_call x1, Pallas kernels, shards(): pl.pallas_call(put_out, out_shape=tuple((jax.ShapeDtypeStruct(shape, f32)...  1.01 us

profile of v4, /device:TPU:0, one launch (start us, length us, event | category | flops | bytes accessed | tf_op | source)
XLA Modules:
  0.0 26.1 jit_solution(6318023627639621339)
XLA Ops:
  1.9 23.1 %trilinear.1 = (f32[256,1024]{1,0:T(8,128)S(1)}, f32[16,1024]{1,0:T(8,128)S(1)}, f32[4,1024]{1,0:T(4,128)S(1)}) custom-call(f32[256,1024]{1,0:T(8,128)} %images.1, f32[16,1024]{1,0:T(8,128)} %texts.1, f32[4,1024]{1,0:T(4,128)} %audio.1, s32[1,256]{1,0:T(1,128)} %bitcast.2, s32[1,256]{1,0:T(1,128)} %bitcast.3, f32[1]{0:T(128)S(6)} %copy.10.scale_in, ...), custom_call_target="tpu_custom_call" | custom-call | tf_op jit(solution)/shard_map/trilinear/pallas_call | solution.py:419
  25.0 1.0 %put_out.1 = (f32[256,1024]{1,0:T(8,128)}, f32[16,1024]{1,0:T(8,128)}, f32[4,1024]{1,0:T(4,128)}) custom-call(f32[256,1024]{1,0:T(8,128)S(1)} %get-tuple-element.6.refs_0_, f32[16,1024]{1,0:T(8,128)S(1)} %get-tuple-element.7.refs_1_, f32[4,1024]{1,0:T(4,128)S(1)} %get-tuple-element.8.refs_2_), custom_call_target="tpu_custom_call" | custom-call | tf_op jit(solution)/shard_map/put_out/pallas_call | solution.py:477
